TPU v7x, 256 devices: a whole 4x4x8 slice. The times are simulated.
256 devices in a mesh: seq: 32 (over y, z), grp: 8 (over x, core).
Axes of the slice: x: 4, y: 4, z: 8, core: 2. Of those that a mesh axis runs over, the one named last changes fastest.
Arguments:
- mixer_input: bfloat16 [5120, 32768], P('grp', 'seq'), may hold values from -5 to 5
- step_sizes: float32 [80, 32768], P('grp', 'seq'), may hold values from 0 to 1, as said below
- decay_rates: float32 [80], P('grp'), may hold values from 1 to 2
- skip_gain: float32 [80], P('grp'), may hold values from 0.5 to 1.5
- input_basis: bfloat16 [32768, 128], P('seq'), may hold values from -5 to 5
- output_basis: bfloat16 [32768, 128], P('seq'), may hold values from -0.5 to 0.5
- out_weight: bfloat16 [5120, 2560], P(None, 'grp'), may hold values from -0.078125 to 0.078125
Outputs:
- layer_output: bfloat16 [32768, 2560], P('seq', 'grp')
Inputs may be any that keep to these rules, and one draw needn't show every extreme that they name: `step_sizes`: positive step sizes.
All inputs are finite; a program needn't handle non-finite values.
Results may differ from a plain program's by a relative error of at most 0.0065.
Values may be sent and summed in bfloat16 or wider, within the bound.
A program may use at most 128 MiB of HBM per device.

v0:
```python
import jax
import jax.numpy as jnp
from jax import lax
from jax.sharding import PartitionSpec as P

HP = 64
N = 128
GROUP = 256


def entering_2(value, axis, combine, identity):
    peers, here = (lax.axis_size(axis), lax.axis_index(axis))
    everything = jax.tree.map(
        lambda part, kind: lax.all_gather(part.astype(kind), axis),
        value,
        (jnp.bfloat16, jnp.bfloat16),
    )
    start = jax.tree.map(
        lambda part, zero: jnp.broadcast_to(jnp.asarray(zero, part.dtype), part.shape),
        value,
        identity,
    )

    def lap(k, before):
        reached = k < here
        new = combine(
            before, jax.tree.map(lambda part, own: part[k].astype(own.dtype), everything, value)
        )
        return jax.tree.map(lambda a, b: jnp.where(reached, a, b), new, before)

    return lax.fori_loop(0, peers, lap, start)


def carry_in(total_log, final_state):
    total_decay = jnp.exp(total_log)

    def combine(earlier, later):
        return (earlier[0] * later[0], later[0][:, None, None] * earlier[1] + later[1])

    identity = (jnp.ones_like(total_decay), jnp.zeros_like(final_state))
    _, carried = entering_2((total_decay, final_state), "seq", combine, identity)
    return carried


def on_device(
    mixer_input, step_sizes, decay_rates, skip_gain, input_basis, output_basis, out_weight
):
    heads_here = step_sizes.shape[0]
    tokens_here = step_sizes.shape[1]
    count = tokens_here // GROUP
    channels = mixer_input.reshape(heads_here, HP, count, GROUP)
    log_decay = -(decay_rates[:, None] * step_sizes).reshape(heads_here, count, GROUP)
    steps_blocked = step_sizes.reshape(heads_here, count, GROUP)
    running = jnp.cumsum(log_decay, axis=2)
    basis_in_blocked = input_basis.reshape(count, GROUP, N)
    basis_out_blocked = output_basis.reshape(count, GROUP, N)
    gram = jnp.einsum(
        "cin,cjn->cij", basis_out_blocked, basis_in_blocked, preferred_element_type=jnp.float32
    )
    rows_index = lax.broadcasted_iota(jnp.int32, (GROUP, GROUP), 0)
    cols_index = lax.broadcasted_iota(jnp.int32, (GROUP, GROUP), 1)
    causal = rows_index >= cols_index
    gaps = running[:, :, :, None] - running[:, :, None, :]
    mixing = jnp.where(
        causal,
        gram[None] * jnp.exp(jnp.where(causal, gaps, 0.0)) * steps_blocked[:, :, None, :],
        0.0,
    ).astype(jnp.bfloat16)
    inner = jnp.einsum("hcij,hpcj->hpci", mixing, channels, preferred_element_type=jnp.float32)
    tail = jnp.exp(running[:, :, -1:] - running) * steps_blocked
    weighted_terms = (basis_in_blocked.astype(jnp.float32)[None] * tail[:, :, :, None]).astype(
        jnp.bfloat16
    )
    summaries = jnp.einsum(
        "hcjn,hpcj->chnp", weighted_terms, channels, preferred_element_type=jnp.float32
    )
    block_decay = jnp.exp(running[:, :, -1])

    def advance(state, pair):
        decay, digest_record = pair
        return (decay[:, None, None] * state + digest_record, state)

    zero_state = jnp.zeros((heads_here, N, HP), jnp.float32)
    final_state, entering = lax.scan(advance, zero_state, (block_decay.T, summaries))
    block_sums = jnp.sum(log_decay, axis=2)
    prefix = jnp.exp(jnp.cumsum(block_sums, axis=1) - block_sums)
    total_log = jnp.sum(block_sums, axis=1)
    basis_out_wide = basis_out_blocked.astype(jnp.float32)
    within = jnp.exp(running)[:, None]
    direct = skip_gain[:, None, None, None] * channels.astype(jnp.float32)
    carried = carry_in(total_log, final_state)
    states = entering + prefix.T[:, :, None, None] * carried[None]
    from_state = jnp.einsum(
        "cin,chnp->hpci", basis_out_wide, states, precision=lax.Precision.HIGHEST
    )
    mixed = inner + from_state * within + direct
    mixed_columns = mixed.astype(jnp.bfloat16).reshape(heads_here * HP, tokens_here)
    result = jnp.einsum(
        "kt,kd->td",
        lax.all_gather(mixed_columns, "grp", axis=0, tiled=True),
        out_weight,
        preferred_element_type=jnp.float32,
    )
    return result.astype(jnp.bfloat16)


def solution(mesh):
    placed = (
        P("grp", "seq"),
        P("grp", "seq"),
        P("grp"),
        P("grp"),
        P("seq", None),
        P("seq", None),
        P(None, "grp"),
    )
    return jax.shard_map(
        on_device, mesh=mesh, in_specs=placed, out_specs=P("seq", "grp"), check_vma=False
    )
```

profile of v0, /device:TPU:1, one launch (start us, length us, event | category | flops | bytes accessed | tf_op | source)
XLA Modules:
  0.0 377.4 jit_solution(3592990008132862632)
XLA Ops:
  14.0 5.1 %reduce-window.6 = f32[10,4,2,128]{3,0,1,2:T(8,128)} reduce-window(f32[10,4,2,128]{3,0,1,2:T(8,128)} %copy.30, f32[]{:T(128)} %constant.47.clone.1), window={size=1x1x1x128 pad=0_0x0_0x0_0x127_0}, to_apply=%region_0.0 | reduce-window | flops 1300480 | bytes 81924 | tf_op jit(solution)/shard_map/reduce-window
  27.5 3.8 %reshape.116 = bf16[10,64,4,256]{3,2,1,0:T(4,128)(2,1)} reshape(bf16[640,1024]{1,0:T(8,128)(2,1)} %param.11) | data formatting | bytes 2621440 | tf_op jit(solution)/shard_map/reshape | solution.py:51
  32.1 5.6 %fusion.9 = f32[4,10,128,64]{3,2,1,0:T(8,128)} fusion(f32[10,4,256]{2,0,1:T(8,128)} %copy.35, f32[4,256,128]{2,1,0:T(8,128)} %convert_element_type.64, bf16[10,64,4,256]{3,2,1,0:T(4,128)(2,1)} %reshape.116), kind=kOutput, calls=%fused_computation.17 | convolution fusion | flops 170393600 | bytes 3186688 | tf_op jit(solution)/shard_map/hcjn,hpcj->chnp/dot_general | solution.py:74
  37.8 15.7 %while.27 = (s32[]{:T(128)}, f32[10,128,64]{2,1,0:T(8,128)}, f32[4,10,128,64]{3,2,1,0:T(8,128)}, f32[4,10]{1,0:T(4,128)S(1)}, f32[4,10,128,64]{3,2,1,0:T(8,128)}, /*index=5*/s32[]{:T(128)}, s32[]{:T(128)}) while((s32[]{:T(128)}, f32[10,128,64]{2,1,0:T(8,128)}, f32[4,10,128,64]{3,2,1,0:T(8,128)}, f32[4,10]{1,0:T(4,128)S(1)}, ...), condition=%wide.region_3.4_spmd.clone, body=%wide.region_2.3_spmd.clone.sunk | while | flops 327683 | bytes 2294488 | solution.py:84
  38.7 2.1 bitcast_add_fusion.2
  40.7 2.0 bitcast_dynamic-update-slice_fusion.2
  42.7 2.3 bitcast_add_fusion.2
  47.0 2.3 bitcast_add_fusion.2
  51.2 2.3 bitcast_add_fusion.2
  58.5 64.9 %all-reduce = bf16[320]{0:T(512)(128)(2,1)S(1)} all-reduce(bf16[320]{0:T(512)(128)(2,1)S(1)} %dynamic-update-slice), channel_id=2, replica_groups=mesh['seq'=32,'grp'=8] {'seq'}, use_global_device_ids=true, to_apply=%add | all-reduce | flops 320 | bytes 1280
  127.2 2.2 fusion.23
  129.4 12.8 %all-gather.7.cloned.1.call-done = bf16[320,128,64]{1,2,0:T(8,128)(2,1)} async-done(((bf16[10,128,64]{1,2,0:T(8,128)(2,1)}), bf16[320,128,64]{1,2,0:T(8,128)(2,1)}) %all-gather.7.cloned.1.call-update) | async-done | bytes 5242896 | tf_op jit(solution)/shard_map/all_gather | solution.py:14
  142.2 149.2 %while.28 = (s32[]{:T(128)}, f32[10,128,64]{2,1,0:T(8,128)}, s32[]{:T(128)}, bf16[32,10]{1,0:T(8,128)(2,1)}, bf16[32,10,128,64]{2,3,1,0:T(8,128)(2,1)}, /*index=5*/s32[]{:T(128)}, s32[]{:T(128)}) while((s32[]{:T(128)}, f32[10,128,64]{2,1,0:T(8,128)}, s32[]{:T(128)}, bf16[32,10]{1,0:T(8,128)(2,1)}, ...), condition=%wide.region_8.9_spmd.clone, body=%wide.region_7.8_spmd.clone.sunk | while | flops 409614 | bytes 1474765 | solution.py:31
  149.2 2.2 fusion.33
  153.8 2.2 fusion.33
  158.5 2.2 fusion.33
  163.1 2.2 fusion.33
  167.8 2.2 fusion.33
  172.5 2.2 fusion.33
  177.1 2.2 fusion.33
  181.8 2.2 fusion.33
  186.5 2.2 fusion.33
  191.2 2.2 fusion.33
  195.9 2.2 fusion.33
  200.6 2.2 fusion.33
  205.2 2.2 fusion.33
  209.9 2.2 fusion.33
  214.6 2.2 fusion.33
  219.3 2.2 fusion.33
  223.9 2.2 fusion.33
  228.5 2.2 fusion.33
  233.2 2.2 fusion.33
  237.8 2.2 fusion.33
  242.5 2.2 fusion.33
  247.1 2.2 fusion.33
  251.7 2.2 fusion.33
  256.4 2.2 fusion.33
  261.1 2.2 fusion.33
  265.8 2.2 fusion.33
  270.5 2.2 fusion.33
  275.1 2.2 fusion.33
  279.8 2.2 fusion.33
  284.5 2.2 fusion.33
  289.2 2.2 fusion.33
  291.4 4.4 %fusion.13 = f32[4,10,64,256]{3,2,0,1:T(8,128)S(1)} fusion(bf16[4,256,128,1]{2,1,0,3:T(8,128)(2,1)} %bitcast.58, f32[4,10,128,64]{3,2,1,0:T(8,128)} %get-tuple-element.127, f32[10,128,64]{2,1,0:T(8,128)} %get-tuple-element.129, f32[4,10]{1,0:T(4,128)S(1)} %copy.38), kind=kOutput, calls=%fused_computation.22 | convolution fusion | flops 1007288320 | bytes 4522144 | tf_op jit(solution)/shard_map/cin,chnp->hpci/dot_general | solution.py:93
  295.9 4.0 %fusion.12 = bf16[10,64,4,256]{3,1,2,0:T(8,128)(2,1)S(1)} fusion(f32[4,10,64,256]{3,2,0,1:T(8,128)S(1)} %fusion.13, f32[10,4,256]{2,1,0:T(4,128)S(1)} %copy-done.6, f32[10,4,256]{2,1,0:T(4,128)S(1)} %copy-done.5, f32[4,256,256]{2,1,0:T(8,128)S(1)} %copy-done.2, pred[256,256]{1,0:T(8,128)(4,1)S(1)} %copy-done.7, bf16[10,64,4,256]{3,2,1,0:T(4,128)(2,1)S(1)} %copy-done.1, ...), kind=kOutput, calls=%fused_computation.21 | convolution fusion | flops 355205120 | bytes 6479912 | tf_op jit(solution)/shard_map/hcij,hpcj->hpci/dot_general | solution.py:69
  302.3 61.1 %all-gather.5.cloned.1.call-done = bf16[5120,1024]{1,0:T(8,128)(2,1)} async-done(((bf16[640,1024]{1,0:T(8,128)(2,1)}), bf16[5120,1024]{1,0:T(8,128)(2,1)}) %all-gather.5.cloned.1.call-update) | async-done | bytes 10485776 | tf_op jit(solution)/shard_map/all_gather | solution.py:100
  363.4 7.2 %convolution_convert_fusion = bf16[1024,320]{0,1:T(8,128)(2,1)} fusion(bf16[5120,320]{0,1:T(8,128)(2,1)S(1)} %copy-done, bf16[5120,1024]{1,0:T(8,128)(2,1)} %all-gather.5.cloned.1.call-done), kind=kOutput, calls=%fused_computation.27 | convolution fusion | flops 3355770880 | bytes 14417920 | tf_op jit(solution)/shard_map/kt,kd->td/dot_general | solution.py:98
  (168 shorter events, 114.1 us)
Async XLA Ops:
  6.5 356.9 %copy-start = (bf16[5120,320]{0,1:T(8,128)(2,1)S(1)}, bf16[5120,320]{0,1:T(8,128)(2,1)}, u32[]{:S(2)}) copy-start(bf16[5120,320]{0,1:T(8,128)(2,1)} %param.17) | copy-start | bytes 9830404
  6.5 24.7 %copy-start.3 = (bf16[1024,128]{1,0:T(8,128)(2,1)S(1)}, bf16[1024,128]{1,0:T(8,128)(2,1)}, u32[]{:S(2)}) copy-start(bf16[1024,128]{1,0:T(8,128)(2,1)} %param.15) | copy-start | bytes 786436
  6.5 135.6 %all-gather.7.cloned.1.call-start = ((), (), s32[]{:S(2)}) async-start(), calls=%async_computation.1 | async-start | bytes 5406720 | tf_op jit(solution)/shard_map/all_gather | solution.py:14
  9.8 0.6 copy-start.4
  37.8 19.2 %copy-start.11 = (u32[256]{0:T(256)S(1)}, u32[256]{0:T(256)}, u32[]{:S(2)}) copy-start(u32[256]{0:T(256)} %constant.56) | copy-start | bytes 3076
  37.8 20.5 %copy-start.9 = (f32[10]{0:T(128)S(1)}, f32[10]{0:T(128)}, u32[]{:S(2)}) copy-start(f32[10]{0:T(128)} %get-tuple-element.206) | copy-start | bytes 124
  55.4 308.0 %all-gather.5.cloned.1.call-start = ((), (), s32[]{:S(2)}) async-start(), calls=%async_computation | async-start | bytes 11796480 | tf_op jit(solution)/shard_map/all_gather | solution.py:100
  291.3 4.5 %copy-start.1 = (bf16[10,64,4,256]{3,2,1,0:T(4,128)(2,1)S(1)}, bf16[10,64,4,256]{3,2,1,0:T(4,128)(2,1)}, u32[]{:S(2)}) copy-start(bf16[10,64,4,256]{3,2,1,0:T(4,128)(2,1)} %reshape.116) | copy-start | bytes 3932164
  291.4 4.5 %copy-start.2 = (f32[4,256,256]{2,1,0:T(8,128)S(1)}, f32[4,256,256]{2,1,0:T(8,128)}, u32[]{:S(2)}) copy-start(f32[4,256,256]{2,1,0:T(8,128)} %fusion.23) | copy-start | bytes 3145732
  291.4 4.5 %copy-start.5 = (f32[10,4,256]{2,1,0:T(4,128)S(1)}, f32[10,4,256]{2,1,0:T(4,128)}, u32[]{:S(2)}) copy-start(f32[10,4,256]{2,1,0:T(4,128)} %reduce_window_sum.42) | copy-start | bytes 122884
  291.4 4.5 %copy-start.6 = (f32[10,4,256]{2,1,0:T(4,128)S(1)}, f32[10,4,256]{2,1,0:T(4,128)}, u32[]{:S(2)}) copy-start(f32[10,4,256]{2,1,0:T(4,128)} %mul.111) | copy-start | bytes 122884
  291.4 4.5 %copy-start.7 = (pred[256,256]{1,0:T(8,128)(4,1)S(1)}, pred[256,256]{1,0:T(8,128)(4,1)}, u32[]{:S(2)}) copy-start(pred[256,256]{1,0:T(8,128)(4,1)} %iota_compare_fusion) | copy-start | bytes 196612
  291.4 4.5 %copy-start.8 = (f32[10,4,256]{2,1,0:T(4,128)S(1)}, f32[10,4,256]{2,1,0:T(4,128)}, u32[]{:S(2)}) copy-start(f32[10,4,256]{2,1,0:T(4,128)} %get-tuple-element.208) | copy-start | bytes 122884
  291.4 4.5 %copy-start.10 = (f32[10]{0:T(128)S(1)}, f32[10]{0:T(128)}, u32[]{:S(2)}) copy-start(f32[10]{0:T(128)} %param.14) | copy-start | bytes 124
Sparse Core Ops, SparseCore 0:
  55.5 86.6 all-gather.6
  302.5 60.9 all-gather.4
where the time goes:
time: 381 us; the launch traced here: 377 us
  other arithmetic  120 us (31%)
  local copies, waits for them, and re-layouts  81.2 us (21%)
  waiting for transfers between devices  73.9 us (19%)
  blocking collectives  64.9 us (17%)
  matrix products  23.5 us (6%)
  between operations  14.2 us (4%)
    select_n x32, other arithmetic, lap(): return jax.tree.map(lambda a, b: jnp.where(reached, a, b), new, before)  68.9 us
    unnamed x1, blocking collectives  64.9 us
    all_gather x1, waiting for transfers between devices, on_device(): lax.all_gather(mixed_columns, 'grp', axis=0, tiled=True)  61.1 us
    dynamic_slice x64, local copies, waits for them, and re-layouts, lap(): part[k].astype(own.dtype)  58.7 us
    convert_element_type x32, other arithmetic, lap(): part[k].astype(own.dtype)  21.4 us
    all_gather x1, waiting for transfers between devices, entering_2(): lax.all_gather(part.astype(kind), axis)  12.8 us
    add x4, other arithmetic, advance(): return (decay[:, None, None] * state + digest_record, state)  8.81 us
  transfers between devices with their start and end apart: 2, of which 2 were waited for; matrix products, arithmetic and copies ran while one was open for 2% of the time, Pallas kernels for 0%

commit v1 on v0

--- a/solution.py
+++ b/solution.py
@@ -1,11 +1,25 @@
+import functools
 import jax
 import jax.numpy as jnp
 from jax import lax
 from jax.sharding import PartitionSpec as P
+from jax.lax import all_to_all, psum
 
 HP = 64
 N = 128
 GROUP = 256
+
+
+def prepare_the_block(frame_in, k_dim):
+    return jnp.concatenate(
+        all_to_all(
+            jnp.stack(tuple((frame_in for _ in range(psum(1, axis_name="grp")))), 0), "grp", 0, 0
+        ),
+        k_dim,
+    )
+
+
+take_teams_all = functools.partial(prepare_the_block, k_dim=0)
 
 
 def entering_2(value, axis, combine, identity):
@@ -96,10 +110,7 @@
     mixed = inner + from_state * within + direct
     mixed_columns = mixed.astype(jnp.bfloat16).reshape(heads_here * HP, tokens_here)
     result = jnp.einsum(
-        "kt,kd->td",
-        lax.all_gather(mixed_columns, "grp", axis=0, tiled=True),
-        out_weight,
-        preferred_element_type=jnp.float32,
+        "kt,kd->td", take_teams_all(mixed_columns), out_weight, preferred_element_type=jnp.float32
     )
     return result.astype(jnp.bfloat16)
 

time: 381 us -> 432 us (1.13)
  blocking collectives: 64.9 us -> 190 us
  waiting for transfers between devices: 73.9 us -> 12.8 us
  other arithmetic: 120 us -> 114 us
  local copies, waits for them, and re-layouts: 81.2 us -> 76.5 us
    all_to_all x0 -> x1, blocking collectives: none -> 125 us  [prepare_the_block(): all_to_all(jnp.stack(tuple((frame_in for _ in range(psum(1, axis_name='gr...]
    all_gather x1 -> x0, waiting for transfers between devices: 61.1 us -> none  [on_device(): lax.all_gather(mixed_columns, 'grp', axis=0, tiled=True)]
  transfers between devices with their start and end apart: 2 -> 1, of which waited for: 2 -> 1; matrix products, arithmetic and copies ran while one was open for 2% -> 2% of each run, Pallas kernels for 0% -> 0%
where the time goes in v1:
time: 432 us; the launch traced here: 429 us
  blocking collectives  190 us (44%)
  other arithmetic  114 us (26%)
  local copies, waits for them, and re-layouts  76.5 us (18%)
  matrix products  20.8 us (5%)
  between operations  14.3 us (3%)
  waiting for transfers between devices  12.8 us (3%)
    all_to_all x1, blocking collectives, prepare_the_block(): all_to_all(jnp.stack(tuple((frame_in for _ in range(psum(1, axis_name='gr...  125 us
    select_n x32, other arithmetic, lap(): return jax.tree.map(lambda a, b: jnp.where(reached, a, b), new, before)  68.9 us
    unnamed x1, blocking collectives  64.9 us
    dynamic_slice x64, local copies, waits for them, and re-layouts, lap(): part[k].astype(own.dtype)  58.7 us
    convert_element_type x32, other arithmetic, lap(): part[k].astype(own.dtype)  20.8 us
    all_gather x1, waiting for transfers between devices, entering_2(): lax.all_gather(part.astype(kind), axis)  12.8 us
    add x4, other arithmetic, advance(): return (decay[:, None, None] * state + digest_record, state)  8.81 us
  transfers between devices with their start and end apart: 1, of which 1 were waited for; matrix products, arithmetic and copies ran while one was open for 2% of the time, Pallas kernels for 0%

profile of v1, /device:TPU:1, one launch (start us, length us, event | category | flops | bytes accessed | tf_op | source)
XLA Modules:
  0.0 428.8 jit_solution(13872664467536664628)
XLA Ops:
  9.3 2.3 reduce-window.6
  14.7 3.8 reshape.118
  18.5 5.6 %fusion.9 = f32[4,10,128,64]{3,2,1,0:T(8,128)} fusion(f32[10,4,256]{2,0,1:T(8,128)S(1)} %copy.35, f32[4,256,128]{2,1,0:T(8,128)} %convert_element_type.64, bf16[10,64,4,256]{3,2,1,0:T(4,128)(2,1)} %reshape.118), kind=kOutput, calls=%fused_computation.17 | convolution fusion | flops 170393600 | bytes 3186688 | tf_op jit(solution)/shard_map/hcjn,hpcj->chnp/dot_general | solution.py:88
  24.1 15.7 %while.27 = (s32[]{:T(128)}, f32[10,128,64]{2,1,0:T(8,128)}, f32[4,10,128,64]{3,2,1,0:T(8,128)}, f32[4,10]{1,0:T(4,128)S(1)}, f32[4,10,128,64]{3,2,1,0:T(8,128)}, /*index=5*/s32[]{:T(128)}, s32[]{:T(128)}) while((s32[]{:T(128)}, f32[10,128,64]{2,1,0:T(8,128)}, f32[4,10,128,64]{3,2,1,0:T(8,128)}, f32[4,10]{1,0:T(4,128)S(1)}, ...), condition=%wide.region_3.4_spmd.clone, body=%wide.region_2.3_spmd.clone.sunk | while | flops 327683 | bytes 2293988 | solution.py:98
  25.1 2.1 bitcast_add_fusion.2
  29.1 2.3 bitcast_add_fusion.2
  33.4 2.3 bitcast_add_fusion.2
  37.6 2.3 bitcast_add_fusion.2
  44.9 64.9 %all-reduce = bf16[320]{0:T(512)(128)(2,1)S(1)} all-reduce(bf16[320]{0:T(512)(128)(2,1)S(1)} %dynamic-update-slice), channel_id=2, replica_groups=mesh['seq'=32,'grp'=8] {'seq'}, use_global_device_ids=true, to_apply=%add | all-reduce | flops 320 | bytes 1280
  113.6 2.2 fusion.23
  115.8 12.8 %all-gather.4.cloned.1.call-done = bf16[320,128,64]{1,2,0:T(8,128)(2,1)} async-done(((bf16[10,128,64]{1,2,0:T(8,128)(2,1)}), bf16[320,128,64]{1,2,0:T(8,128)(2,1)}) %all-gather.4.cloned.1.call-update) | async-done | bytes 5242896 | tf_op jit(solution)/shard_map/all_gather | solution.py:28
  128.6 148.6 %while.28 = (s32[]{:T(128)}, f32[10,128,64]{2,1,0:T(8,128)}, s32[]{:T(128)}, bf16[32,10]{1,0:T(8,128)(2,1)}, bf16[32,10,128,64]{2,3,1,0:T(8,128)(2,1)}, /*index=5*/s32[]{:T(128)}, s32[]{:T(128)}) while((s32[]{:T(128)}, f32[10,128,64]{2,1,0:T(8,128)}, s32[]{:T(128)}, bf16[32,10]{1,0:T(8,128)(2,1)}, ...), condition=%wide.region_8.9_spmd.clone, body=%wide.region_7.8_spmd.clone.sunk | while | flops 409614 | bytes 1474773 | solution.py:45
  135.6 2.2 fusion.33
  140.3 2.2 fusion.33
  145.0 2.2 fusion.33
  149.7 2.2 fusion.33
  154.3 2.2 fusion.33
  159.0 2.2 fusion.33
  163.7 2.2 fusion.33
  168.3 2.2 fusion.33
  172.9 2.2 fusion.33
  177.6 2.2 fusion.33
  182.2 2.2 fusion.33
  186.8 2.2 fusion.33
  191.4 2.2 fusion.33
  196.0 2.2 fusion.33
  200.6 2.2 fusion.33
  205.3 2.2 fusion.33
  210.0 2.2 fusion.33
  214.7 2.2 fusion.33
  219.4 2.2 fusion.33
  224.0 2.2 fusion.33
  228.7 2.2 fusion.33
  233.4 2.2 fusion.33
  238.1 2.2 fusion.33
  242.7 2.2 fusion.33
  247.3 2.2 fusion.33
  251.9 2.2 fusion.33
  256.5 2.2 fusion.33
  261.1 2.2 fusion.33
  265.8 2.2 fusion.33
  270.4 2.2 fusion.33
  275.0 2.2 fusion.33
  277.2 4.5 %fusion.13 = f32[4,10,64,256]{3,2,0,1:T(8,128)S(1)} fusion(bf16[4,256,128,1]{2,1,0,3:T(8,128)(2,1)} %bitcast.60, f32[4,10,128,64]{3,2,1,0:T(8,128)} %get-tuple-element.127, f32[10,128,64]{2,1,0:T(8,128)} %get-tuple-element.129, f32[4,10]{1,0:T(4,128)S(1)} %copy.38), kind=kOutput, calls=%fused_computation.22 | convolution fusion | flops 1007288320 | bytes 4522144 | tf_op jit(solution)/shard_map/cin,chnp->hpci/dot_general | solution.py:107
  281.7 4.0 fusion.12
  287.0 5.3 %stack.3 = bf16[8,640,1024]{2,1,0:T(8,128)(2,1)} broadcast(bf16[640,1024]{1,0:T(8,128)(2,1)S(1)} %bitcast.56), dimensions={1,2} | broadcast | bytes 11796480 | tf_op jit(solution)/shard_map/stack | solution.py:16
  292.3 125.1 %all_to_all.5 = bf16[8,640,1024]{2,1,0:T(8,128)(2,1)S(1)} all-to-all(bf16[8,640,1024]{2,1,0:T(8,128)(2,1)} %stack.3), channel_id=1, replica_groups=mesh['seq'=32,'grp'=8] {'grp'}, dimensions={0} | all-to-all | bytes 20971520 | tf_op jit(solution)/shard_map/all_to_all | solution.py:15
  417.4 4.5 %convolution_convert_fusion = bf16[1024,320]{0,1:T(8,128)(2,1)} fusion(bf16[5120,320]{0,1:T(8,128)(2,1)S(1)} %copy-done, bf16[5120,1024]{1,0:T(8,128)(2,1)S(1)} %bitcast.54), kind=kOutput, calls=%fused_computation.27 | convolution fusion | flops 3355770880 | bytes 14417920 | tf_op jit(solution)/shard_map/kt,kd->td/dot_general | solution.py:112
  (169 shorter events, 103.6 us)
Async XLA Ops:
  6.5 410.9 %copy-start = (bf16[5120,320]{0,1:T(8,128)(2,1)S(1)}, bf16[5120,320]{0,1:T(8,128)(2,1)}, u32[]{:S(2)}) copy-start(bf16[5120,320]{0,1:T(8,128)(2,1)} %param.17) | copy-start | bytes 9830404
  6.5 122.0 %all-gather.4.cloned.1.call-start = ((), (), s32[]{:S(2)}) async-start(), calls=%async_computation.1 | async-start | bytes 5406720 | tf_op jit(solution)/shard_map/all_gather | solution.py:28
  7.6 16.6 %copy-start.7 = (f32[10,4,256]{2,1,0:T(4,128)}, f32[10,4,256]{2,1,0:T(4,128)S(1)}, u32[]{:S(2)}) copy-start(f32[10,4,256]{2,1,0:T(4,128)S(1)} %mul.111) | copy-start | bytes 122884
  8.6 0.6 copy-start.4
  12.0 12.1 %copy-start.5 = (f32[10,4,256]{2,1,0:T(4,128)}, f32[10,4,256]{2,1,0:T(4,128)S(1)}, u32[]{:S(2)}) copy-start(f32[10,4,256]{2,1,0:T(4,128)S(1)} %reduce_window_sum.42) | copy-start | bytes 122884
  24.1 19.1 %copy-start.12 = (u32[256]{0:T(256)S(1)}, u32[256]{0:T(256)}, u32[]{:S(2)}) copy-start(u32[256]{0:T(256)} %constant.56) | copy-start | bytes 3076
  24.1 89.4 %copy-start.3 = (bf16[1024,128]{1,0:T(8,128)(2,1)S(1)}, bf16[1024,128]{1,0:T(8,128)(2,1)}, u32[]{:S(2)}) copy-start(bf16[1024,128]{1,0:T(8,128)(2,1)} %param.15) | copy-start | bytes 786436
  277.1 4.5 %copy-start.1 = (bf16[10,64,4,256]{3,2,1,0:T(4,128)(2,1)S(1)}, bf16[10,64,4,256]{3,2,1,0:T(4,128)(2,1)}, u32[]{:S(2)}) copy-start(bf16[10,64,4,256]{3,2,1,0:T(4,128)(2,1)} %reshape.118) | copy-start | bytes 3932164
  277.1 4.5 %copy-start.2 = (f32[4,256,256]{2,1,0:T(8,128)S(1)}, f32[4,256,256]{2,1,0:T(8,128)}, u32[]{:S(2)}) copy-start(f32[4,256,256]{2,1,0:T(8,128)} %fusion.23) | copy-start | bytes 3145732
  277.1 4.5 %copy-start.6 = (f32[10,4,256]{2,1,0:T(4,128)S(1)}, f32[10,4,256]{2,1,0:T(4,128)}, u32[]{:S(2)}) copy-start(f32[10,4,256]{2,1,0:T(4,128)} %copy-done.5) | copy-start | bytes 122884
  277.1 4.5 %copy-start.8 = (f32[10,4,256]{2,1,0:T(4,128)S(1)}, f32[10,4,256]{2,1,0:T(4,128)}, u32[]{:S(2)}) copy-start(f32[10,4,256]{2,1,0:T(4,128)} %copy-done.7) | copy-start | bytes 122884
  277.1 4.5 %copy-start.9 = (pred[256,256]{1,0:T(8,128)(4,1)S(1)}, pred[256,256]{1,0:T(8,128)(4,1)}, u32[]{:S(2)}) copy-start(pred[256,256]{1,0:T(8,128)(4,1)} %iota_compare_fusion) | copy-start | bytes 196612
  277.2 4.5 %copy-start.10 = (f32[10,4,256]{2,1,0:T(4,128)S(1)}, f32[10,4,256]{2,1,0:T(4,128)}, u32[]{:S(2)}) copy-start(f32[10,4,256]{2,1,0:T(4,128)} %get-tuple-element.208) | copy-start | bytes 122884
  277.2 4.5 %copy-start.11 = (f32[10]{0:T(128)S(1)}, f32[10]{0:T(128)}, u32[]{:S(2)}) copy-start(f32[10]{0:T(128)} %param.14) | copy-start | bytes 124
Sparse Core Ops, SparseCore 0:
  41.9 86.6 all-gather.3
